TPU v7x, 256 devices: a whole 4x4x8 slice. The times are simulated.
256 devices in a mesh: frames: 8 (over y, x_lo), labels: 8 (over z), hidden: 4 (over x_hi, core).
Axes of the slice: x: 4 (x_hi: 2, x_lo: 2; x = x_hi * 2 + x_lo), y: 4, z: 8, core: 2. Of those that a mesh axis runs over, the one named last changes fastest.
Arguments:
- features: bfloat16 [1024, 1024], P('frames'), may hold values from -6 to 6
- up_weight: bfloat16 [1024, 4096], P(None, 'hidden'), may hold values from -0.1875 to 0.1875
- down_weight: bfloat16 [4096, 640], P('hidden'), may hold values from -0.09375 to 0.09375
- predictor: bfloat16 [512, 640], P(('labels', 'hidden')), may hold values from -4 to 4
- out_weight: bfloat16 [640, 1024], replicated, may hold values from -1.1 to 1.1
- blank_weight: float32 [1024, 512], P('frames', ('labels', 'hidden')), may hold values from 0 to 0.06
- label_weight: float32 [1024, 512], P('frames', ('labels', 'hidden')), may hold values from 0 to 0.06
- targets: int32 [512], P(('labels', 'hidden')), may hold values from 1 to 1023
Outputs:
- enc_grad: float32 [1024, 640], P(('frames', 'labels', 'hidden'))
- pred_grad: float32 [512, 640], P(('labels', 'hidden'))
- head_grad: float32 [1024, 640], P(('frames', 'labels', 'hidden'))
All inputs are finite; a program needn't handle non-finite values.
Results may differ from a plain program's by a relative error of at most 0.0023.
Values sent between devices are 32-bit elements; how exact they have to be, the bound alone decides.
A program may use at most 64 MiB of HBM per device.

v0:
```python
import math
import jax
import jax.numpy as jnp
from jax import lax
from jax.sharding import PartitionSpec as P


def on_device(
    features, up_weight, down_weight, predictor, out_weight, blank_weight, label_weight, targets
):
    frames_dev = features.shape[0]
    labels_dev = predictor.shape[0]
    joint_width = predictor.shape[1]
    vocab_size = out_weight.shape[1]
    hidden_act = jax.nn.relu(
        jnp.dot(features, up_weight, preferred_element_type=jnp.float32)
    ).astype(jnp.bfloat16)
    partial_enc = jnp.dot(hidden_act, down_weight, preferred_element_type=jnp.float32)
    encoded = lax.psum(partial_enc, "hidden")
    block_rows = min(frames_dev, max(1, 512 // labels_dev))
    while frames_dev % block_rows:
        block_rows = block_rows - 1
    pred_wide = predictor.astype(jnp.float32)
    vocab_ids = jnp.arange(vocab_size, dtype=jnp.int32)
    label_hot = (targets[:, None] == vocab_ids[None, :]).astype(jnp.float32)
    blank_hot = (vocab_ids == 0).astype(jnp.float32)
    cell_hot = jnp.broadcast_to(label_hot[None], (block_rows, labels_dev, vocab_size)).reshape(
        -1, vocab_size
    )

    def joint_step(pred_sum, inputs):
        enc_block, blank_block, label_block = inputs
        joint_cells = jnp.tanh(enc_block[:, None, :] + pred_wide[None, :, :]).astype(jnp.bfloat16)
        joint_cells = joint_cells.reshape(block_rows * labels_dev, joint_width)
        logits = jnp.dot(joint_cells, out_weight, preferred_element_type=jnp.float32)
        top_logit = jnp.max(logits, axis=1, keepdims=True)
        log_total = top_logit + jnp.log(jnp.sum(jnp.exp(logits - top_logit), axis=1, keepdims=True))
        probs = jnp.exp(logits - log_total)
        blank_flat = blank_block.reshape(-1, 1)
        label_flat = label_block.reshape(-1, 1)
        logit_grad = (
            (blank_flat + label_flat) * probs - blank_flat * blank_hot - label_flat * cell_hot
        ).astype(jnp.bfloat16)
        joint_grad = lax.dot_general(
            logit_grad, out_weight, (((1,), (1,)), ((), ())), preferred_element_type=jnp.float32
        )
        cells_wide = joint_cells.astype(jnp.float32)
        tanh_grad = (joint_grad * (1.0 - cells_wide * cells_wide)).reshape(
            block_rows, labels_dev, joint_width
        )
        return (
            pred_sum + jnp.sum(tanh_grad, axis=0),
            (joint_cells, logit_grad, jnp.sum(tanh_grad, axis=1)),
        )

    inputs = (
        encoded.reshape(-1, block_rows, joint_width),
        blank_weight.reshape(-1, block_rows, labels_dev),
        label_weight.reshape(-1, block_rows, labels_dev),
    )
    pred_sum, stacked = lax.scan(
        joint_step, jnp.zeros((labels_dev, joint_width), jnp.float32), inputs
    )
    joint_all = stacked[0].reshape(-1, joint_width)
    grad_all = stacked[1].reshape(-1, vocab_size)
    enc_parts = stacked[2].reshape(frames_dev, joint_width)
    enc_grad = lax.psum_scatter(enc_parts, ("labels", "hidden"), scatter_dimension=0, tiled=True)
    pred_grad = lax.psum(pred_sum, "frames")
    n_frames = lax.axis_size("frames")
    n_group = lax.axis_size("labels") * lax.axis_size("hidden")
    total_cells = frames_dev * n_frames * labels_dev * n_group
    head_sum = lax.psum_scatter(
        lax.dot_general(
            grad_all, joint_all, (((0,), (0,)), ((), ())), preferred_element_type=jnp.float32
        ),
        ("frames", "labels", "hidden"),
        scatter_dimension=0,
        tiled=True,
    )
    return (enc_grad, pred_grad, head_sum / math.sqrt(total_cells))


def solution(mesh):
    placed = (
        P("frames", None),
        P(None, "hidden"),
        P("hidden", None),
        P(("labels", "hidden"), None),
        P(),
        P("frames", ("labels", "hidden")),
        P("frames", ("labels", "hidden")),
        P(("labels", "hidden")),
    )
    return jax.shard_map(
        on_device,
        mesh=mesh,
        in_specs=placed,
        out_specs=(
            P(("frames", "labels", "hidden"), None),
            P(("labels", "hidden"), None),
            P(("frames", "labels", "hidden"), None),
        ),
        check_vma=False,
    )
```

profile of v0, /device:TPU:2, one launch (start us, length us, event | category | flops | bytes accessed | tf_op | source)
XLA Modules:
  0.0 650.8 jit_solution(10384635351723706598)
XLA Ops:
  7.3 1.5 copy-done
  8.8 2.8 fusion.8
  12.0 48.1 %all-reduce.6.cloned.1.call-done = f32[4,32,640]{2,1,0:T(8,128)} async-done(((f32[4,32,640]{2,1,0:T(8,128)}), f32[4,32,640]{2,1,0:T(8,128)}) %all-reduce.6.cloned.1.call-update) | async-done | bytes 327696 | tf_op jit(solution)/shard_map/psum | solution.py:19
  60.1 56.8 %while.17 = (s32[]{:T(128)}, f32[16,640]{1,0:T(8,128)S(1)}, bf16[4,512,640]{2,1,0:T(8,128)(2,1)}, bf16[4,512,1024]{2,1,0:T(8,128)(2,1)}, f32[4,32,640]{2,1,0:T(8...) while((s32[]{:T(128)}, f32[16,640]{1,0:T(8,128)S(1)}, ...), condition=%wide.region_6.7_spmd.clone, body=%wide.region_1.6_spmd.clone.sunk | while | flops 1350033408 | bytes 32403152 | solution.py:61
  61.3 2.4 fusion.33
  65.8 3.4 bitcast_dynamic-update-slice_fusion.6
  69.2 2.2 bitcast_reduce_fusion.2
  72.0 1.4 reduce_sum.37
  75.5 2.4 fusion.33
  80.0 3.4 bitcast_dynamic-update-slice_fusion.6
  83.4 2.1 bitcast_reduce_fusion.2
  86.2 1.4 reduce_sum.37
  89.7 2.4 fusion.33
  94.2 3.4 bitcast_dynamic-update-slice_fusion.6
  97.6 2.2 bitcast_reduce_fusion.2
  100.4 1.4 reduce_sum.37
  103.9 2.4 fusion.33
  108.4 3.4 bitcast_dynamic-update-slice_fusion.6
  111.8 2.2 bitcast_reduce_fusion.2
  114.6 1.4 reduce_sum.37
  117.0 8.0 %convolution_bitcast_fusion = f32[1024,640]{1,0:T(8,128)} fusion(bf16[4,512,1024]{2,1,0:T(8,128)(2,1)} %get-tuple-element.70, bf16[4,512,640]{2,1,0:T(8,128)(2,1)} %get-tuple-element.71), kind=kOutput, calls=%fused_computation.19 | convolution fusion | flops 2684354560 | bytes 9437184 | tf_op jit(solution)/shard_map/dot_general | solution.py:73
  127.0 31.7 %psum.15 = f32[16,640]{1,0:T(8,128)} all-reduce(f32[16,640]{1,0:T(8,128)S(1)} %get-tuple-element.69), channel_id=1, replica_groups=mesh['frames'=8,'labels'=8,'hidden'=4] {'frames'}, use_global_device_ids=true, to_apply=%region_8.9 | all-reduce | flops 10240 | bytes 81920 | tf_op jit(solution)/shard_map/psum | solution.py:68
  158.7 214.1 %all-reduce.8.cloned.1.call-done = f32[128,640]{1,0:T(8,128)} async-done(((f32[128,640]{1,0:T(8,128)}), f32[128,640]{1,0:T(8,128)}) %all-reduce.8.cloned.1.call-update) | async-done | bytes 327696
  374.1 268.8 %all-reduce.10.cloned.1.call-done = f32[1024,640]{1,0:T(8,128)} async-done(((f32[1024,640]{1,0:T(8,128)}), f32[1024,640]{1,0:T(8,128)}) %all-reduce.10.cloned.1.call-update) | async-done | bytes 2621456
  (92 shorter events, 23.6 us)
Async XLA Ops:
  7.2 1.6 copy-start
  7.2 4.5 copy-start.4
  7.2 4.6 copy-start.5
  7.2 4.7 copy-start.3
  7.2 4.7 copy-start.6
  7.2 52.9 %all-reduce.6.cloned.1.call-start = ((), (), s32[]{:S(2)}) async-start(), calls=%async_computation | async-start | bytes 655360 | tf_op jit(solution)/shard_map/psum | solution.py:19
  11.6 361.2 %all-reduce.8.cloned.1.call-start = ((), (), s32[]{:S(2)}) async-start(), calls=%async_computation.1 | async-start | bytes 655360
  63.7 1.4 copy-start.1
  65.8 3.4 copy-start.2
  77.9 1.4 copy-start.1
  80.0 3.5 copy-start.2
  92.1 1.4 copy-start.1
  94.2 3.4 copy-start.2
  106.3 1.4 copy-start.1
  108.4 3.4 copy-start.2
  117.0 526.0 %all-reduce.10.cloned.1.call-start = ((), (), s32[]{:S(2)}) async-start(), calls=%async_computation.2 | async-start | bytes 5242880
  125.1 0.7 copy-start.7
Sparse Core Ops, SparseCore 0:
  11.7 48.3 all-reduce.5
  117.1 255.6 all-reduce.7
  378.2 264.6 all-reduce.9
where the time goes:
time: 652 us; the launch traced here: 651 us
  waiting for transfers between devices  531 us (81%)
  blocking collectives  31.7 us (5%)
  matrix products  29 us (4%)
  other arithmetic  23.8 us (4%)
  local copies, waits for them, and re-layouts  20.3 us (3%)
  between operations  14.5 us (2%)
    unnamed x5, waiting for transfers between devices  483 us
    psum x1, waiting for transfers between devices, on_device(): encoded = lax.psum(partial_enc, 'hidden')  48.1 us
    psum x1, blocking collectives, on_device(): pred_grad = lax.psum(pred_sum, 'frames')  31.7 us
    dynamic_update_slice x4, other arithmetic, on_device(): lax.scan(joint_step, jnp.zeros((labels_dev, joint_width), jnp.float32), i...  13.6 us
  transfers between devices with their start and end apart: 3, of which 3 were waited for; matrix products, arithmetic and copies ran while one was open for 2% of the time, Pallas kernels for 0%

commit v1 on v0

--- a/solution.py
+++ b/solution.py
@@ -16,7 +16,8 @@
         jnp.dot(features, up_weight, preferred_element_type=jnp.float32)
     ).astype(jnp.bfloat16)
     partial_enc = jnp.dot(hidden_act, down_weight, preferred_element_type=jnp.float32)
-    encoded = lax.psum(partial_enc, "hidden")
+    parts = lax.all_gather(partial_enc, "hidden")
+    encoded = jnp.sum(parts, axis=0)
     block_rows = min(frames_dev, max(1, 512 // labels_dev))
     while frames_dev % block_rows:
         block_rows = block_rows - 1

time: 652 us -> 627 us (0.962)
  waiting for transfers between devices: 531 us -> 509 us
    psum x1 -> x0, waiting for transfers between devices: 48.1 us -> none  [on_device(): encoded = lax.psum(partial_enc, 'hidden')]
    all_gather x0 -> x1, waiting for transfers between devices: none -> 26.5 us  [on_device(): parts = lax.all_gather(partial_enc, 'hidden')]
where the time goes in v1:
time: 627 us
  waiting for transfers between devices  509 us (81%)
  blocking collectives  31.8 us (5%)
  matrix products  29 us (5%)
  other arithmetic  25.2 us (4%)
  local copies, waits for them, and re-layouts  16.8 us (3%)
  between operations  14.5 us (2%)
    unnamed x5, waiting for transfers between devices  483 us
    psum x1, blocking collectives, on_device(): pred_grad = lax.psum(pred_sum, 'frames')  31.8 us
    all_gather x1, waiting for transfers between devices, on_device(): parts = lax.all_gather(partial_enc, 'hidden')  26.5 us
    dynamic_update_slice x4, other arithmetic, on_device(): lax.scan(joint_step, jnp.zeros((labels_dev, joint_width), jnp.float32), i...  13.6 us
  transfers between devices with their start and end apart: 3, of which 3 were waited for; matrix products, arithmetic and copies ran while one was open for 2% of the time, Pallas kernels for 0%

profile of v1, /device:TPU:2, one launch (start us, length us, event | category | flops | bytes accessed | tf_op | source)
XLA Modules:
  0.0 626.7 jit_solution(15514025350204765328)
XLA Ops:
  7.3 1.5 copy-done
  8.8 2.9 fusion.8
  12.1 26.5 %all-gather.3.cloned.1.call-done = f32[512,640]{1,0:T(8,128)} async-done(((f32[128,640]{1,0:T(8,128)}), f32[512,640]{1,0:T(8,128)}) %all-gather.3.cloned.1.call-update) | async-done | bytes 1310736 | tf_op jit(solution)/shard_map/all_gather | solution.py:19
  38.6 1.4 reduce_sum.36
  40.0 53.2 %while.17 = (s32[]{:T(128)}, f32[16,640]{1,0:T(8,128)S(1)}, bf16[4,512,640]{2,1,0:T(8,128)(2,1)}, bf16[4,512,1024]{2,1,0:T(8,128)(2,1)}, f32[4,32,640]{2,1,0:T(8...) while((s32[]{:T(128)}, f32[16,640]{1,0:T(8,128)S(1)}, ...), condition=%wide.region_6.7_spmd.clone, body=%wide.region_1.6_spmd.clone.sunk | while | flops 1350033408 | bytes 32403152 | solution.py:62
  40.3 2.4 fusion.33
  44.8 3.4 bitcast_dynamic-update-slice_fusion.6
  48.2 2.2 bitcast_reduce_fusion.2
  51.0 1.4 reduce_sum.47
  53.6 2.4 fusion.33
  58.1 3.4 bitcast_dynamic-update-slice_fusion.6
  61.6 2.2 bitcast_reduce_fusion.2
  64.3 1.4 reduce_sum.47
  66.9 2.4 fusion.33
  71.4 3.4 bitcast_dynamic-update-slice_fusion.6
  74.8 2.2 bitcast_reduce_fusion.2
  77.6 1.4 reduce_sum.47
  80.2 2.4 fusion.33
  84.7 3.4 bitcast_dynamic-update-slice_fusion.6
  88.1 2.2 bitcast_reduce_fusion.2
  93.3 8.0 %convolution_bitcast_fusion = f32[1024,640]{1,0:T(8,128)} fusion(bf16[4,512,1024]{2,1,0:T(8,128)(2,1)} %get-tuple-element.70, bf16[4,512,640]{2,1,0:T(8,128)(2,1)} %get-tuple-element.71), kind=kOutput, calls=%fused_computation.19 | convolution fusion | flops 2684354560 | bytes 9437184 | tf_op jit(solution)/shard_map/dot_general | solution.py:74
  103.3 31.8 %psum.7 = f32[16,640]{1,0:T(8,128)} all-reduce(f32[16,640]{1,0:T(8,128)S(1)} %get-tuple-element.69), channel_id=1, replica_groups=mesh['frames'=8,'labels'=8,'hidden'=4] {'frames'}, use_global_device_ids=true, to_apply=%region_8.9 | all-reduce | flops 10240 | bytes 81920 | tf_op jit(solution)/shard_map/psum | solution.py:69
  135.0 213.7 %all-reduce.5.cloned.1.call-done = f32[128,640]{1,0:T(8,128)} async-done(((f32[128,640]{1,0:T(8,128)}), f32[128,640]{1,0:T(8,128)}) %all-reduce.5.cloned.1.call-update) | async-done | bytes 327696
  350.1 268.8 %all-reduce.7.cloned.1.call-done = f32[1024,640]{1,0:T(8,128)} async-done(((f32[1024,640]{1,0:T(8,128)}), f32[1024,640]{1,0:T(8,128)}) %all-reduce.7.cloned.1.call-update) | async-done | bytes 2621456
  (93 shorter events, 21.4 us)
Async XLA Ops:
  7.2 1.6 copy-start
  7.2 4.6 copy-start.4
  7.2 4.7 copy-start.5
  7.2 4.8 copy-start.3
  7.2 4.8 copy-start.6
  7.2 31.4 %all-gather.3.cloned.1.call-start = ((), (), s32[]{:S(2)}) async-start(), calls=%async_computation | async-start | bytes 1638400 | tf_op jit(solution)/shard_map/all_gather | solution.py:19
  11.7 337.1 %all-reduce.5.cloned.1.call-start = ((), (), s32[]{:S(2)}) async-start(), calls=%async_computation.1 | async-start | bytes 655360
  42.7 1.4 copy-start.1
  44.8 3.4 copy-start.2
  56.0 1.4 copy-start.1
  58.1 3.5 copy-start.2
  69.3 1.4 copy-start.1
  71.4 3.4 copy-start.2
  82.6 1.4 copy-start.1
  84.7 3.4 copy-start.2
  93.3 525.6 %all-reduce.7.cloned.1.call-start = ((), (), s32[]{:S(2)}) async-start(), calls=%async_computation.2 | async-start | bytes 5242880
  101.4 0.7 copy-start.7
Sparse Core Ops, SparseCore 0:
  11.8 26.7 all-gather.2
  93.4 255.2 all-reduce.4
  354.2 264.6 all-reduce.6
